TPU v7x, 128 devices: a whole 4x4x4 slice. The times are simulated.
128 devices in a mesh: rows: 32 (over y, z, core), grp: 4 (over x).
Axes of the slice: x: 4, y: 4, z: 4, core: 2. Of those that a mesh axis runs over, the one named last changes fastest.
Arguments:
- start: float32 [256, 262144], P('grp', 'rows'), may hold values from -50 to 50
- momenta: float32 [256, 262144], P('grp', 'rows'), may hold values from -6 to 6
- observed: float32 [262144], P('rows'), may hold values from -6 to 6
- precision_obs: float32 [262144], P('rows'), may hold values from 0.5 to 4
- blocks: float32 [2048, 4, 128, 128], P('rows'), may hold values from -0.08 to 9
- block_cols: int32 [2048, 4], P('rows'), may hold values from 0 to 2047, as said below
- block_count: int32 [2048], P('rows'), may hold values from 2 to 4, as said below
- step_size: float32 [1], replicated, may hold values from 0.2 to 0.3
- trajectory: float32 [256], P('grp'), may hold values from 0.3 to 1.5
Outputs:
- position: float32 [256, 262144], P('grp', 'rows')
- momentum: float32 [256, 262144], P('grp', 'rows')
- chees: float32 [256], P('grp')
Inputs may be any that keep to these rules, and one draw needn't show every extreme that they name: `block_cols`: slot 0 of block row r names r; slots 1 to 3 name distinct block rows r + k modulo 2048 with k from 1 to 64, and k = 64 occurs. `block_count`: 4 is reached.
All inputs are finite; a program needn't handle non-finite values.
Results may differ from a plain program's by a relative error of at most 0.0003.
Values sent between devices are 32-bit elements; how exact they have to be, the bound alone decides.
A program may use at most 192 MiB of HBM per device.

v0:
```python
import functools

import jax
import jax.numpy as jnp
from jax import lax
from jax.experimental import pallas as pl
from jax.experimental.pallas import tpu as pltpu
from jax.sharding import PartitionSpec as P

F32 = jnp.float32
BF16 = jnp.bfloat16
I32 = jnp.int32
NN = (((1,), (0,)), ((), ()))

SIDE = 128
SLOTS = 4
OFF = SLOTS - 1
BANDS = 64
CELLS = BANDS * SIDE
EDGES = BANDS * OFF
CHUNKS = 2
CH = 32
PIECES = 4
PB = BANDS // PIECES
PE = EDGES // PIECES
LOAD = 4
NLOAD = BANDS // LOAD
NSTAGE = 4


def dot(a, b):
    return lax.dot_general(a, b, NN, preferred_element_type=F32)


def split_rows(x):
    high = x.astype(BF16)
    low = (x - high.astype(F32)).astype(BF16)
    return jnp.concatenate([high, low], axis=0)


def split_lanes(x):
    high = x.astype(BF16)
    low = (x - high.astype(F32)).astype(BF16)
    return jnp.concatenate([high, low], axis=1)


def joined(p):
    return (p[:CH, :SIDE] + p[:CH, SIDE:]) + p[CH:, :SIDE]


def lanes(r):
    return pl.ds(pl.multiple_of(r * SIDE, SIDE), SIDE)


def edge_tables(cols_ref, count_ref, first, nblocks, table_ref):
    total = BANDS * SLOTS
    count = count_ref[...]
    sub = lax.broadcasted_iota(I32, (BANDS, BANDS), 0)
    lane = lax.broadcasted_iota(I32, (BANDS, BANDS), 1)
    row_id = lax.broadcasted_iota(I32, (1, BANDS), 1)
    col_id = lax.broadcasted_iota(I32, (BANDS, 1), 0)

    def column(row):
        return jnp.sum(jnp.where(sub == lane, row, 0), axis=1, keepdims=True)

    local, dest_col, key_row, key_col = [], [], [], []
    for s in range(1, SLOTS):
        d = cols_ref[s : s + 1, :] - first
        d = jnp.where(d < 0, d + nblocks, d)
        local.append(jnp.minimum(d, 2 * BANDS - 1))
        live = jnp.where(s < count, d, 0)
        key = live * total + row_id * OFF + (s - 1)
        dest_col.append(column(live))
        key_row.append(key)
        key_col.append(column(key))
    place = lax.broadcasted_iota(I32, (BANDS, total), 1)
    edge = jnp.zeros((1, total), I32)
    band = jnp.zeros((1, total), I32)
    dest = jnp.zeros((1, total), I32)
    before = jnp.zeros((1, total), I32)
    upto = jnp.zeros((1, total), I32)
    found = jnp.zeros((1, total), I32)

    def down(x):
        return jnp.sum(x, axis=0, keepdims=True)

    for s in range(OFF):
        rank = jnp.zeros((BANDS, 1), I32)
        for k in range(OFF):
            rank += jnp.sum(jnp.where(key_row[k] > key_col[s], 1, 0), axis=1, keepdims=True)
        here = rank == place
        edge += down(jnp.where(here, col_id * OFF + s, 0))
        band += down(jnp.where(here, col_id, 0))
        dest += down(jnp.where(here, dest_col[s], 0))
        before += down(jnp.where(rank + 1 == place, dest_col[s], 0))
        upto += down(jnp.where(dest_col[s] >= place, 1, 0))
        found += down(jnp.where(dest_col[s] == place, 1, 0))
    table_ref[0:1, :] = edge
    table_ref[1:2, :] = band
    table_ref[2:3, :] = jnp.where(dest == before, 1, 0)
    table_ref[3:4, :] = jnp.maximum(upto - 1, 0)
    table_ref[4:5, :] = jnp.minimum(found, 1)
    pad = jnp.zeros((1, total - BANDS), I32)
    for s in range(OFF):
        table_ref[5 + s : 6 + s, :] = jnp.concatenate([local[s], pad], axis=1)


def kernel(
    nrows,
    ngrp,
    chain_total,
    all_cells,
    start_hbm,
    momenta_hbm,
    observed_hbm,
    precision_hbm,
    blocks_hbm,
    cols_ref,
    count_ref,
    count_smem,
    step_smem,
    trajectory_ref,
    position_hbm,
    momentum_hbm,
    chees_ref,
    stage,
    flat,
    turned,
    v,
    m,
    split,
    u,
    sums,
    sent,
    next_v,
    carried,
    obs,
    prec,
    cell_sums,
    cell_all,
    mean,
    acc,
    part,
    part_y,
    table,
    smem,
    stage_sem,
    load_sem,
    out_sem,
    table_sem,
    up_send,
    up_recv,
    dn_send,
    dn_recv,
    x_send,
    x_recv,
    a_send,
    a_recv,
    b_send,
    b_recv,
):
    me = lax.axis_index("rows")
    grp = lax.axis_index("grp")
    up = lax.rem(me + nrows - 1, nrows)
    down = lax.rem(me + 1, nrows)
    near = 8
    far = nrows // near
    in_near = lax.rem(me, near)
    base = me - in_near
    in_far = me // near

    def near_peer(d):
        return base + lax.rem(in_near + d, near)

    def far_peer(d):
        return lax.rem(me + near * d, nrows)

    def load_v(c):
        return pltpu.make_async_copy(start_hbm.at[pl.ds(c * CH, CH)], v.at[c], load_sem.at[c])

    def load_m(c):
        return pltpu.make_async_copy(momenta_hbm.at[pl.ds(c * CH, CH)], m.at[c], load_sem.at[2 + c])

    load_obs = pltpu.make_async_copy(observed_hbm, obs, load_sem.at[4])
    load_prec = pltpu.make_async_copy(precision_hbm, prec, load_sem.at[5])

    def load_blocks(i):
        slot = lax.rem(i, NSTAGE)
        rows = pl.ds(i * LOAD * SLOTS, LOAD * SLOTS)
        return pltpu.make_async_copy(blocks_hbm.at[rows], stage.at[slot], stage_sem.at[slot])

    def store_position(c):
        return pltpu.make_async_copy(v.at[c], position_hbm.at[pl.ds(c * CH, CH)], out_sem.at[0, c])

    def store_momentum(c):
        return pltpu.make_async_copy(m.at[c], momentum_hbm.at[pl.ds(c * CH, CH)], out_sem.at[1, c])

    def send_up(g, c):
        par = lax.rem(g, 2)
        return pltpu.make_async_remote_copy(
            v.at[c], next_v.at[par, c], up_send.at[c], up_recv.at[par, c], device_id={"rows": up}
        )

    def send_down(g, c, p):
        par = lax.rem(g, 2)
        cells = pl.ds(pl.multiple_of(p * (PB * SIDE), PB * SIDE), PB * SIDE)
        return pltpu.make_async_remote_copy(
            sent.at[c, :, cells],
            carried.at[par, c, :, cells],
            dn_send.at[c, p],
            dn_recv.at[par, c, p],
            device_id={"rows": down},
        )

    def send_sums(which, d):
        return pltpu.make_async_remote_copy(
            cell_sums.at[which],
            cell_all.at[which, grp],
            x_send.at[which, d],
            x_recv.at[which, grp],
            device_id={"grp": lax.rem(grp + d, ngrp)},
        )

    def take_sums(which, d):
        slot = lax.rem(grp + d, ngrp)
        return pltpu.make_async_remote_copy(
            cell_sums.at[which],
            cell_all.at[which, slot],
            x_send.at[which, d],
            x_recv.at[which, slot],
            device_id={"grp": slot},
        )

    for c in range(CHUNKS):
        load_v(c).start()
    for i in range(NSTAGE):
        load_blocks(i).start()
    load_obs.start()
    load_prec.start()
    for c in range(CHUNKS):
        load_m(c).start()

    barrier = pltpu.get_barrier_semaphore()
    for peer in (up, down):
        pl.semaphore_signal(barrier, inc=1, device_id={"rows": peer})
    for d in range(1, ngrp):
        pl.semaphore_signal(barrier, inc=1, device_id={"grp": lax.rem(grp + d, ngrp)})
    for d in range(1, near):
        pl.semaphore_signal(barrier, inc=1, device_id={"rows": near_peer(d)})
    for d in range(1, far):
        pl.semaphore_signal(barrier, inc=1, device_id={"rows": far_peer(d)})

    edge_tables(cols_ref, count_ref, me * BANDS, nrows * BANDS, table)
    to_smem = pltpu.make_async_copy(table, smem, table_sem)
    to_smem.start()

    pl.semaphore_wait(barrier, 2 + (ngrp - 1) + (near - 1) + (far - 1))

    for c in range(CHUNKS):
        load_v(c).wait()
        send_up(0, c).start()

    def first_cells(r, _):
        total = jnp.zeros((1, SIDE), F32)
        for c in range(CHUNKS):
            x = v[c, :, lanes(r)]
            total += jnp.sum(x, axis=0, keepdims=True)
            split[c, r] = split_rows(x)
        cell_sums[0, pl.ds(r, 1), :] = total
        return 0

    lax.fori_loop(0, BANDS, first_cells, 0, unroll=4)
    for d in range(1, ngrp):
        send_sums(0, d).start()

    def take_blocks(i, _):
        load_blocks(i).wait()
        slot = lax.rem(i, NSTAGE)
        for k in range(LOAD):
            r = i * LOAD + k
            count = count_smem[r]
            for s in range(SLOTS):
                b = stage[slot, k * SLOTS + s]
                if s >= 2:
                    b = jnp.where(s < count, b, 0.0)
                pair = split_lanes(b)
                if s == 0:
                    turned[r, 0:SIDE, :] = pair
                else:
                    flat[r * OFF + (s - 1)] = pair

        @pl.when(i + NSTAGE < NLOAD)
        def _():
            load_blocks(i + NSTAGE).start()

        return 0

    lax.fori_loop(0, NLOAD, take_blocks, 0)
    to_smem.wait()

    def lower(g, c):
        def piece(q, total):
            p = PIECES - 1 - q

            def edge(k, total):
                place = q * PE + k
                term = joined(dot(split[c, smem[1, place]], flat[smem[0, place]]))
                total = jnp.where(smem[2, place] != 0, total, 0.0) + term
                sums[place] = total
                return total

            total = lax.fori_loop(0, PE, edge, total, unroll=16)

            def place_out(j, _):
                r = p * PB + j
                x = sums[smem[3, BANDS + r]]
                sent[c, :, lanes(r)] = jnp.where(smem[4, BANDS + r] != 0, x, 0.0)
                return 0

            lax.fori_loop(0, PB, place_out, 0, unroll=8)
            send_down(g, c, p).start()
            return total

        lax.fori_loop(0, PIECES, piece, jnp.zeros((CH, SIDE), F32))

        def place_own(r, _):
            x = sums[smem[3, r]]
            u[c, :, lanes(r)] = jnp.where(smem[4, r] != 0, x, 0.0)
            return 0

        lax.fori_loop(0, BANDS, place_own, 0, unroll=8)

    def first_lower(c, _):
        lower(0, c)
        return 0

    lax.fori_loop(0, CHUNKS, first_lower, 0)

    def turn(r, _):
        for s in range(OFF):
            x = flat[r * OFF + s]
            rows = pl.ds((s + 1) * SIDE, SIDE)
            turned[r, rows, :] = jnp.concatenate([x[:, :SIDE].T, x[:, SIDE:].T], axis=1)
        return 0

    lax.fori_loop(0, BANDS, turn, 0, unroll=2)

    def means(which):
        for d in range(1, ngrp):
            take_sums(which, d).wait_recv()
        cell_all[which, grp] = cell_sums[which]
        total = cell_all[which, 0]
        for k in range(1, ngrp):
            total = total + cell_all[which, k]
        mean[which] = total / chain_total

    def spread(which):
        for c in range(CHUNKS):

            def add(r, total):
                x = v[c, :, lanes(r)] - mean[which, pl.ds(r, 1), :]
                return total + x * x

            acc[which, c] = lax.fori_loop(0, BANDS, add, jnp.zeros((CH, SIDE), F32), unroll=8)

    means(0)
    spread(0)
    for c in range(CHUNKS):
        load_m(c).wait()
    load_obs.wait()
    load_prec.wait()

    step = step_smem[0]

    def upper(g, c):
        par = lax.rem(g, 2)
        send_up(g, c).wait_recv()

        def take(r, _):
            split[c, BANDS + r] = split_rows(next_v[par, c, :, lanes(r)])
            return 0

        lax.fori_loop(0, BANDS, take, 0, unroll=8)

        def row(r, _):
            rows = [split[c, r]] + [split[c, smem[5 + s, r]] for s in range(OFF)]
            term = joined(dot(jnp.concatenate(rows, axis=1), turned[r]))
            u[c, :, lanes(r)] = u[c, :, lanes(r)] + term
            return 0

        lax.fori_loop(0, BANDS, row, 0, unroll=8)

    def gradient(g, c, r):
        par = lax.rem(g, 2)
        x = v[c, :, lanes(r)]
        pull = prec[pl.ds(r, 1), :] * (x - obs[pl.ds(r, 1), :])
        return x, -(u[c, :, lanes(r)] + carried[par, c, :, lanes(r)]) - pull

    def move(g, c):
        kick = jnp.where(g == 0, step / 2, step)
        send_up(g, c).wait_send()

        def piece(q, _):
            p = PIECES - 1 - q
            send_down(g, c, p).wait_recv()

            def band(j, _):
                r = p * PB + j
                x, grad = gradient(g, c, r)
                mom = m[c, :, lanes(r)] + kick * grad
                m[c, :, lanes(r)] = mom
                x = x + step * mom
                v[c, :, lanes(r)] = x
                split[c, r] = split_rows(x)
                here = jnp.sum(x, axis=0, keepdims=True)
                old = jnp.where(c == 0, 0.0, cell_sums[1, pl.ds(r, 1), :])
                cell_sums[1, pl.ds(r, 1), :] = old + here
                return 0

            return lax.fori_loop(0, PB, band, 0, unroll=4)

        lax.fori_loop(0, PIECES, piece, 0)

    def finish(g, c):
        send_up(g, c).wait_send()

        def piece(q, total):
            p = PIECES - 1 - q
            send_down(g, c, p).wait_recv()

            def band(j, total):
                r = p * PB + j
                x, grad = gradient(g, c, r)
                mom = m[c, :, lanes(r)] + (step / 2) * grad
                m[c, :, lanes(r)] = mom
                return total + (x - mean[1, pl.ds(r, 1), :]) * mom

            return lax.fori_loop(0, PB, band, total, unroll=4)

        acc[2, c] = lax.fori_loop(0, PIECES, piece, jnp.zeros((CH, SIDE), F32))

    def stage_of(t, _):
        g = t // CHUNKS
        c = lax.rem(t, CHUNKS)
        upper(g, c)

        @pl.when(g < 2)
        def _():
            move(g, c)
            send_up(g + 1, c).start()

            @pl.when(g == 1)
            def _():
                store_position(c).start()

            for p in range(PIECES):
                send_down(g, c, p).wait_send()
            lower(g + 1, c)

        @pl.when(t == 3)
        def _():
            for d in range(1, ngrp):
                send_sums(1, d).start()

        @pl.when(t == 4)
        def _():
            means(1)

        @pl.when(g == 2)
        def _():
            finish(g, c)
            store_momentum(c).start()

        @pl.when(t == 4)
        def _():
            spread(1)

        return 0

    lax.fori_loop(0, 3 * CHUNKS, stage_of, 0)

    sub = lax.broadcasted_iota(I32, (CH, SIDE), 0)
    lane = lax.broadcasted_iota(I32, (CH, SIDE), 1)
    inner = jnp.zeros((1, SIDE), F32)
    change = jnp.zeros((1, SIDE), F32)
    for c in range(CHUNKS):
        here = lane == sub + c * CH
        column = jnp.sum(acc[2, c], axis=1, keepdims=True)
        inner += jnp.sum(jnp.where(here, column, 0.0), axis=0, keepdims=True)
        column = jnp.sum(acc[1, c], axis=1, keepdims=True) - jnp.sum(acc[0, c], axis=1, keepdims=True)
        change += jnp.sum(jnp.where(here, column, 0.0), axis=0, keepdims=True)
    own = jnp.concatenate([inner, change, jnp.zeros((6, SIDE), F32)], axis=0)

    def near_copy(slot, d):
        return pltpu.make_async_remote_copy(
            part.at[in_near], part.at[slot], a_send.at[d], a_recv.at[slot], device_id={"rows": near_peer(d)}
        )

    def far_copy(slot, d):
        return pltpu.make_async_remote_copy(
            part_y.at[in_far], part_y.at[slot], b_send.at[d], b_recv.at[slot], device_id={"rows": far_peer(d)}
        )

    part[in_near] = own
    for d in range(1, near):
        near_copy(in_near, d).start()
    for d in range(1, near):
        near_copy(lax.rem(in_near + d, near), d).wait_recv()
    total = part[0]
    for k in range(1, near):
        total = total + part[k]
    part_y[in_far] = total
    for d in range(1, far):
        far_copy(in_far, d).start()
    for d in range(1, far):
        far_copy(lax.rem(in_far + d, far), d).wait_recv()
    total = part_y[0]
    for k in range(1, far):
        total = total + part_y[k]
    chees_ref[...] = (
        trajectory_ref[...] * (total[1:2, : CHUNKS * CH] / all_cells) * (total[0:1, : CHUNKS * CH] / all_cells)
    )

    for d in range(1, near):
        near_copy(in_near, d).wait_send()
    for d in range(1, far):
        far_copy(in_far, d).wait_send()
    for which in range(2):
        for d in range(1, ngrp):
            send_sums(which, d).wait_send()
    for c in range(CHUNKS):
        for p in range(PIECES):
            send_down(2, c, p).wait_send()
        store_position(c).wait()
        store_momentum(c).wait()


def on_device(start, momenta, observed, precision_obs, blocks, block_cols, block_count, step_size, trajectory):
    nrows = lax.axis_size("rows")
    ngrp = lax.axis_size("grp")
    far = nrows // 8
    hbm = pl.BlockSpec(memory_space=pl.ANY)
    vmem = pl.BlockSpec(memory_space=pltpu.VMEM)
    smem = pl.BlockSpec(memory_space=pltpu.SMEM)
    dma = pltpu.SemaphoreType.DMA
    chains = CHUNKS * CH
    position, momentum, chees = pl.pallas_call(
        functools.partial(kernel, nrows, ngrp, chains * ngrp, CELLS * nrows),
        out_shape=(
            jax.ShapeDtypeStruct((chains, CELLS), F32),
            jax.ShapeDtypeStruct((chains, CELLS), F32),
            jax.ShapeDtypeStruct((1, chains), F32),
        ),
        in_specs=[hbm, hbm, hbm, hbm, hbm, vmem, vmem, smem, smem, vmem],
        out_specs=(hbm, hbm, vmem),
        scratch_shapes=[
            pltpu.VMEM((NSTAGE, LOAD * SLOTS, SIDE, SIDE), F32),
            pltpu.VMEM((EDGES, SIDE, 2 * SIDE), BF16),
            pltpu.VMEM((BANDS, SLOTS * SIDE, 2 * SIDE), BF16),
            pltpu.VMEM((CHUNKS, CH, CELLS), F32),
            pltpu.VMEM((CHUNKS, CH, CELLS), F32),
            pltpu.VMEM((CHUNKS, 2 * BANDS, 2 * CH, SIDE), BF16),
            pltpu.VMEM((CHUNKS, CH, CELLS), F32),
            pltpu.VMEM((EDGES, CH, SIDE), F32),
            pltpu.VMEM((CHUNKS, CH, CELLS), F32),
            pltpu.VMEM((2, CHUNKS, CH, CELLS), F32),
            pltpu.VMEM((2, CHUNKS, CH, CELLS), F32),
            pltpu.VMEM((BANDS, SIDE), F32),
            pltpu.VMEM((BANDS, SIDE), F32),
            pltpu.VMEM((2, BANDS, SIDE), F32),
            pltpu.VMEM((2, ngrp, BANDS, SIDE), F32),
            pltpu.VMEM((2, BANDS, SIDE), F32),
            pltpu.VMEM((3, CHUNKS, CH, SIDE), F32),
            pltpu.VMEM((8, 8, SIDE), F32),
            pltpu.VMEM((far, 8, SIDE), F32),
            pltpu.VMEM((8, SLOTS * BANDS), I32),
            pltpu.SMEM((8, SLOTS * BANDS), I32),
            dma((NSTAGE,)),
            dma((6,)),
            dma((2, CHUNKS)),
            dma,
            dma((CHUNKS,)),
            dma((2, CHUNKS)),
            dma((CHUNKS, PIECES)),
            dma((2, CHUNKS, PIECES)),
            dma((2, ngrp)),
            dma((2, ngrp)),
            dma((8,)),
            dma((8,)),
            dma((far,)),
            dma((far,)),
        ],
        compiler_params=pltpu.CompilerParams(
            collective_id=0, has_side_effects=True, vmem_limit_bytes=60 * 1024 * 1024
        ),
    )(
        start,
        momenta,
        observed.reshape(BANDS, SIDE),
        precision_obs.reshape(BANDS, SIDE),
        blocks.reshape(BANDS * SLOTS, SIDE, SIDE),
        block_cols.T,
        block_count.reshape(1, BANDS),
        block_count,
        step_size,
        trajectory.reshape(1, chains),
    )
    return position, momentum, chees.reshape(chains)


def solution(mesh):
    placed = (
        P("grp", "rows"),
        P("grp", "rows"),
        P("rows"),
        P("rows"),
        P("rows", None, None, None),
        P("rows", None),
        P("rows"),
        P(),
        P("grp"),
    )
    return jax.shard_map(
        on_device,
        mesh=mesh,
        in_specs=placed,
        out_specs=(P("grp", "rows"), P("grp", "rows"), P("grp")),
        check_vma=False,
    )
```

profile of v0, /device:TPU:1, one launch (start us, length us, event | category | flops | bytes accessed | tf_op | source)
XLA Modules:
  0.0 100.5 jit_solution(12040935110635223562)
XLA Ops:
  1.3 94.1 %shard_map.112 = (f32[64,8192]{1,0:T(8,128)}, f32[64,8192]{1,0:T(8,128)}, f32[1,64]{1,0:T(1,128)}) custom-call(f32[64,8192]{1,0:T(8,128)} %start_hbm.1, f32[64,8192]{1,0:T(8,128)} %momenta_hbm.1, f32[64,128]{1,0:T(8,128)} %bitcast.8, f32[64,128]{1,0:T(8,128)} %bitcast.9, f32[256,128,128]{2,1,0:T(8,128)} %bitcast.7, s32[4,64]{1,0:T(4,128)} %bitcast.10, ...), custom_call_target="tpu_custom_call" | custom-call | tf_op jit(solution)/shard_map/pallas_call | solution.py:547
  95.4 0.0 copy-start
  95.4 3.2 %copy.16 = f32[64,8192]{1,0:T(8,128)} copy(f32[64,8192]{1,0:T(8,128)} %get-tuple-element.12) | data formatting | bytes 4194304
  98.6 0.0 copy-done
  98.6 0.0 copy-start.1
  98.6 1.3 %copy.17 = f32[64,8192]{1,0:T(8,128)} copy(f32[64,8192]{1,0:T(8,128)S(1)} %copy-done) | data formatting | bytes 4194304
  99.9 0.0 copy-done.1
  99.9 0.5 copy.18
Async XLA Ops:
  95.4 3.2 %copy-start = (f32[64,8192]{1,0:T(8,128)S(1)}, f32[64,8192]{1,0:T(8,128)}, u32[]{:S(2)}) copy-start(f32[64,8192]{1,0:T(8,128)} %get-tuple-element.13) | copy-start | bytes 6291460
  98.6 1.3 %copy-start.1 = (f32[1,64]{1,0:T(1,128)S(1)}, f32[1,64]{1,0:T(1,128)}, u32[]{:S(2)}) copy-start(f32[1,64]{1,0:T(1,128)} %get-tuple-element.8) | copy-start | bytes 772
where the time goes:
time: 101 us; the launch traced here: 100 us
  Pallas kernels  94.1 us (93%)
  local copies, waits for them, and re-layouts  5.05 us (5%)
  between operations  1.3 us (1%)
    pallas_call x1, Pallas kernels, on_device(): pl.pallas_call(functools.partial(kernel, nrows, ngrp, chains * ngrp, CELL...  94.1 us
    unnamed x7, local copies, waits for them, and re-layouts  5.05 us

commit v1 on v0

v1 whole, which is shorter than its diff:
```python
import functools

import jax
import jax.numpy as jnp
from jax import lax
from jax.experimental import pallas as pl
from jax.experimental.pallas import tpu as pltpu
from jax.sharding import PartitionSpec as P

F32 = jnp.float32
BF16 = jnp.bfloat16
I32 = jnp.int32
NN = (((1,), (0,)), ((), ()))

SIDE = 128
SLOTS = 4
OFF = SLOTS - 1
BANDS = 64
CELLS = BANDS * SIDE
EDGES = BANDS * OFF
CHUNKS = 2
CH = 32
PIECES = 4
PB = BANDS // PIECES
PE = EDGES // PIECES
LOAD = 4
NLOAD = BANDS // LOAD
NSTAGE = 4
STRIPS = 4


def dot(a, b):
    return lax.dot_general(a, b, NN, preferred_element_type=F32)


def split_rows(x):
    high = x.astype(BF16)
    low = (x - high.astype(F32)).astype(BF16)
    return jnp.concatenate([high, low], axis=0)


def split_lanes(x):
    high = x.astype(BF16)
    low = (x - high.astype(F32)).astype(BF16)
    return jnp.concatenate([high, low], axis=1)


def joined(p):
    return (p[:CH, :SIDE] + p[:CH, SIDE:]) + p[CH:, :SIDE]


def joined_both(p):
    return jnp.concatenate([joined(p[c * 2 * CH : (c + 1) * 2 * CH]) for c in range(CHUNKS)], axis=0)


def lanes(r):
    return pl.ds(pl.multiple_of(r * SIDE, SIDE), SIDE)


def edge_tables(cols_ref, count_ref, first, nblocks, table_ref):
    total = BANDS * SLOTS
    count = count_ref[...]
    sub = lax.broadcasted_iota(I32, (BANDS, BANDS), 0)
    lane = lax.broadcasted_iota(I32, (BANDS, BANDS), 1)
    row_id = lax.broadcasted_iota(I32, (1, BANDS), 1)
    col_id = lax.broadcasted_iota(I32, (BANDS, 1), 0)

    def column(row):
        return jnp.sum(jnp.where(sub == lane, row, 0), axis=1, keepdims=True)

    local, dest_col, key_row, key_col = [], [], [], []
    for s in range(1, SLOTS):
        d = cols_ref[s : s + 1, :] - first
        d = jnp.where(d < 0, d + nblocks, d)
        local.append(jnp.minimum(d, 2 * BANDS - 1))
        live = jnp.where(s < count, d, 0)
        key = (row_id // PB) * (1 << 20) + live * total + row_id * OFF + (s - 1)
        dest_col.append(column(live))
        key_row.append(key)
        key_col.append(column(key))
    place = lax.broadcasted_iota(I32, (BANDS, total), 1)
    edge = jnp.zeros((1, total), I32)
    band = jnp.zeros((1, total), I32)
    dest = jnp.zeros((1, total), I32)
    before = jnp.zeros((1, total), I32)

    def down(x):
        return jnp.sum(x, axis=0, keepdims=True)

    for s in range(OFF):
        rank = jnp.zeros((BANDS, 1), I32)
        for k in range(OFF):
            rank += jnp.sum(jnp.where(key_row[k] > key_col[s], 1, 0), axis=1, keepdims=True)
        here = rank == place
        edge += down(jnp.where(here, col_id * OFF + s, 0))
        band += down(jnp.where(here, col_id, 0))
        dest += down(jnp.where(here, dest_col[s], 0))
        before += down(jnp.where(rank + 1 == place, dest_col[s], 0))
    table_ref[0:1, :] = edge
    table_ref[1:2, :] = band
    table_ref[2:3, :] = jnp.where(dest == before, 1, 0)
    pad = jnp.zeros((1, total - BANDS), I32)
    for s in range(OFF):
        table_ref[3 + s : 4 + s, :] = jnp.concatenate([local[s], pad], axis=1)
    spot = lax.broadcasted_iota(I32, (PB, total), 1)
    spot = jnp.where(spot < SIDE, spot, spot - SIDE)
    side = lax.broadcasted_iota(I32, (1, total), 1)
    for q in range(PIECES):
        upto = jnp.zeros((1, total), I32)
        found = jnp.zeros((1, total), I32)
        for s in range(OFF):
            d = dest_col[s][q * PB : (q + 1) * PB, :]
            upto += down(jnp.where(d >= spot, 1, 0))
            found += down(jnp.where(d == spot, 1, 0))
        last = jnp.maximum(upto - 1, 0)
        table_ref[6 + q : 7 + q, :] = jnp.where(side < SIDE, last, jnp.minimum(found, 1))


def kernel(
    nrows,
    ngrp,
    chain_total,
    all_cells,
    start_hbm,
    momenta_hbm,
    observed_hbm,
    precision_hbm,
    blocks_hbm,
    cols_ref,
    count_ref,
    count_smem,
    step_smem,
    trajectory_ref,
    position_hbm,
    momentum_hbm,
    chees_ref,
    stage,
    flat,
    turned,
    v,
    m,
    split,
    u,
    sums,
    next_v,
    carried,
    obs,
    prec,
    cell_sums,
    cell_all,
    mean,
    mean_next,
    acc,
    part,
    part_y,
    table,
    smem,
    stage_sem,
    load_sem,
    out_sem,
    momentum_sem,
    table_sem,
    up_send,
    up_recv,
    dn_send,
    dn_recv,
    x_send,
    x_recv,
    a_send,
    a_recv,
    b_send,
    b_recv,
    mean_send,
    mean_recv,
):
    me = lax.axis_index("rows")
    grp = lax.axis_index("grp")
    up = lax.rem(me + nrows - 1, nrows)
    down = lax.rem(me + 1, nrows)
    near = 8
    far = nrows // near
    in_near = lax.rem(me, near)
    base = me - in_near
    in_far = me // near

    def near_peer(d):
        return base + lax.rem(in_near + d, near)

    def far_peer(d):
        return lax.rem(me + near * d, nrows)

    def piece_cells(p):
        return pl.ds(pl.multiple_of(p * (PB * SIDE), PB * SIDE), PB * SIDE)

    def load_v(c):
        return pltpu.make_async_copy(start_hbm.at[pl.ds(c * CH, CH)], v.at[c], load_sem.at[c])

    def load_m(c):
        return pltpu.make_async_copy(momenta_hbm.at[pl.ds(c * CH, CH)], m.at[c], load_sem.at[2 + c])

    load_obs = pltpu.make_async_copy(observed_hbm, obs, load_sem.at[4])
    load_prec = pltpu.make_async_copy(precision_hbm, prec, load_sem.at[5])

    def load_band(i):
        per = PB // LOAD
        return ((PIECES - 1 - i // per) * per + lax.rem(i, per)) * LOAD

    def load_blocks(i):
        slot = lax.rem(i, NSTAGE)
        rows = pl.ds(load_band(i) * SLOTS, LOAD * SLOTS)
        return pltpu.make_async_copy(blocks_hbm.at[rows], stage.at[slot], stage_sem.at[slot])

    def store_position(c):
        return pltpu.make_async_copy(v.at[c], position_hbm.at[pl.ds(c * CH, CH)], out_sem.at[c])

    def store_momentum(c, p):
        cells = piece_cells(p)
        return pltpu.make_async_copy(
            m.at[c, :, cells], momentum_hbm.at[pl.ds(c * CH, CH), cells], momentum_sem.at[c, p]
        )

    def send_up(g, c, p):
        par = lax.rem(g, 2)
        return pltpu.make_async_remote_copy(
            v.at[c, :, piece_cells(p)],
            next_v.at[par, c, :, piece_cells(p)],
            up_send.at[c, p],
            up_recv.at[par, c, p],
            device_id={"rows": up},
        )

    def send_down(g, c, p):
        par = lax.rem(g, 2)
        return pltpu.make_async_remote_copy(
            u.at[c, :, pl.ds(pl.multiple_of(CELLS + p * (PB * SIDE), PB * SIDE), PB * SIDE)],
            carried.at[par, c, :, piece_cells(p)],
            dn_send.at[c, p],
            dn_recv.at[par, c, p],
            device_id={"rows": down},
        )

    def send_sums(which, d):
        return pltpu.make_async_remote_copy(
            cell_sums.at[which],
            cell_all.at[which, grp],
            x_send.at[which, d],
            x_recv.at[which, grp],
            device_id={"grp": lax.rem(grp + d, ngrp)},
        )

    def take_sums(which, d):
        slot = lax.rem(grp + d, ngrp)
        return pltpu.make_async_remote_copy(
            cell_sums.at[which],
            cell_all.at[which, slot],
            x_send.at[which, d],
            x_recv.at[which, slot],
            device_id={"grp": slot},
        )

    send_mean = pltpu.make_async_remote_copy(
        mean.at[1], mean_next, mean_send, mean_recv, device_id={"rows": up}
    )

    for c in range(CHUNKS):
        load_v(c).start()
    for i in range(NSTAGE):
        load_blocks(i).start()
    load_obs.start()
    load_prec.start()

    barrier = pltpu.get_barrier_semaphore()
    for peer in (up, down):
        pl.semaphore_signal(barrier, inc=1, device_id={"rows": peer})
    for d in range(1, ngrp):
        pl.semaphore_signal(barrier, inc=1, device_id={"grp": lax.rem(grp + d, ngrp)})
    for d in range(1, near):
        pl.semaphore_signal(barrier, inc=1, device_id={"rows": near_peer(d)})
    for d in range(1, far):
        pl.semaphore_signal(barrier, inc=1, device_id={"rows": far_peer(d)})

    pl.semaphore_wait(barrier, 2 + (ngrp - 1) + (near - 1) + (far - 1))

    for c in range(CHUNKS):
        load_v(c).wait()
        for p in range(PIECES):
            send_up(0, c, p).start()

    edge_tables(cols_ref, count_ref, me * BANDS, nrows * BANDS, table)
    to_smem = pltpu.make_async_copy(table, smem, table_sem)
    to_smem.start()

    def first_cells(r, _):
        total = jnp.zeros((1, SIDE), F32)
        for c in range(CHUNKS):
            x = v[c, :, lanes(r)]
            total += jnp.sum(x, axis=0, keepdims=True)
            split[c, r] = split_rows(x)
        cell_sums[0, pl.ds(r, 1), :] = total
        return 0

    lax.fori_loop(0, BANDS, first_cells, 0, unroll=4)
    for d in range(1, ngrp):
        send_sums(0, d).start()

    def take_blocks(i, _):
        load_blocks(i).wait()
        slot = lax.rem(i, NSTAGE)
        for k in range(LOAD):
            r = load_band(i) + k
            count = count_smem[r]
            for s in range(SLOTS):
                b = stage[slot, k * SLOTS + s]
                if s >= 2:
                    b = jnp.where(s < count, b, 0.0)
                pair = split_lanes(b)
                if s == 0:
                    turned[r, 0:SIDE, :] = pair
                else:
                    flat[r * OFF + (s - 1)] = pair

        @pl.when(i + NSTAGE < NLOAD)
        def _():
            load_blocks(i + NSTAGE).start()

        return 0

    to_smem.wait()

    def spread_out(chunks, p):
        def found(r, i):
            x = sums[smem[6 + p, r], i * CH : (i + 1) * CH, :]
            return jnp.where(smem[6 + p, SIDE + r] != 0, x, 0.0)

        def fresh(j, _):
            r = p * PB + j
            for i, c in enumerate(chunks):
                u[c, :, lanes(r)] = found(r, i)
            return 0

        def more(j, _):
            r = p * PB + j
            for i, c in enumerate(chunks):
                u[c, :, lanes(r)] = u[c, :, lanes(r)] + found(r, i)
            return 0

        lax.fori_loop(0, PB, fresh, 0, unroll=8)

        @pl.when(p == PIECES - 1)
        def _():
            lax.fori_loop(PB, PB + BANDS, fresh, 0, unroll=8)

        @pl.when(p < PIECES - 1)
        def _():
            lax.fori_loop(PB, PB + BANDS, more, 0, unroll=8)

    def quarter(g, c, p):
        def edge(k, total):
            place = (PIECES - 1 - p) * PE + k
            term = joined(dot(split[c, smem[1, place]], flat[smem[0, place]]))
            total = jnp.where(smem[2, place] != 0, total, 0.0) + term
            sums[k, :CH, :] = total
            return total

        place = (PIECES - 1 - p) * PE
        total = joined(dot(split[c, smem[1, place]], flat[smem[0, place]]))
        sums[0, :CH, :] = total
        lax.fori_loop(1, PE, edge, total, unroll=PE - 1)
        spread_out((c,), p)
        send_down(g, c, p).start()

    def first_quarter(q, _):
        p = PIECES - 1 - q
        per = NLOAD // PIECES
        lax.fori_loop(q * per, (q + 1) * per, take_blocks, 0)

        def edges(i, total):
            r = p * PB + i
            for s in range(OFF):
                place = q * PE + i * OFF + s
                band = smem[1, place]
                both = jnp.concatenate([split[c, band] for c in range(CHUNKS)], axis=0)
                term = joined_both(dot(both, flat[smem[0, place]]))
                keep = smem[2, place]
                if s == 0:
                    keep = jnp.where(i == 0, 0, keep)
                total = jnp.where(keep != 0, total, 0.0) + term
                sums[i * OFF + s] = total
                x = flat[r * OFF + s]
                turned[r, (s + 1) * SIDE : (s + 2) * SIDE, :] = jnp.concatenate(
                    [x[:, :SIDE].T, x[:, SIDE:].T], axis=1
                )
            return total

        lax.fori_loop(0, PB, edges, jnp.zeros((CHUNKS * CH, SIDE), F32), unroll=8)
        spread_out(range(CHUNKS), p)
        send_down(0, 0, p).start()
        return 0

    lax.fori_loop(0, PIECES, first_quarter, 0)
    for c in range(CHUNKS):
        load_m(c).start()
    for p in reversed(range(PIECES)):
        send_down(0, 1, p).start()

    def means(which):
        for d in range(1, ngrp):
            take_sums(which, d).wait_recv()
        cell_all[which, grp] = cell_sums[which]
        total = cell_all[which, 0]
        for k in range(1, ngrp):
            total = total + cell_all[which, k]
        mean[which] = total / chain_total

    def spread(which):
        for c in range(CHUNKS):

            def add(r, total):
                x = v[c, :, lanes(r)] - mean[which, pl.ds(r, 1), :]
                return total + x * x

            acc[which, c] = lax.fori_loop(0, BANDS, add, jnp.zeros((CH, SIDE), F32), unroll=8)

    means(0)
    spread(0)
    for c in range(CHUNKS):
        load_m(c).wait()
    load_obs.wait()
    load_prec.wait()

    step = step_smem[0]

    def upper(g, c):
        par = lax.rem(g, 2)

        def piece(p, _):
            send_up(g, c, p).wait_recv()

            def take(j, _):
                r = p * PB + j
                split[c, BANDS + r] = split_rows(next_v[par, c, :, lanes(r)])
                return 0

            lax.fori_loop(0, PB, take, 0, unroll=8)

            def row(j, _):
                r = p * PB + j
                rows = [split[c, r]] + [split[c, smem[3 + s, r]] for s in range(OFF)]
                term = joined(dot(jnp.concatenate(rows, axis=1), turned[r]))
                u[c, :, lanes(r)] = u[c, :, lanes(r)] + term
                return 0

            return lax.fori_loop(0, PB, row, 0, unroll=PB)

        lax.fori_loop(0, PIECES, piece, 0)

    def gradient(g, c, r):
        par = lax.rem(g, 2)
        x = v[c, :, lanes(r)]
        pull = prec[pl.ds(r, 1), :] * (x - obs[pl.ds(r, 1), :])
        return x, -(u[c, :, lanes(r)] + carried[par, c, :, lanes(r)]) - pull

    def move(g, c):
        kick = jnp.where(g == 0, step / 2, step)
        for p in range(PIECES):
            send_up(g, c, p).wait_send()

        def piece(q, _):
            p = PIECES - 1 - q
            send_down(g, c, p).wait_recv()

            def band(j, _):
                r = p * PB + j
                x, grad = gradient(g, c, r)
                mom = m[c, :, lanes(r)] + kick * grad
                m[c, :, lanes(r)] = mom
                x = x + step * mom
                v[c, :, lanes(r)] = x
                split[c, r] = split_rows(x)
                here = jnp.sum(x, axis=0, keepdims=True)
                old = jnp.where(c == 0, 0.0, cell_sums[1, pl.ds(r, 1), :])
                cell_sums[1, pl.ds(r, 1), :] = old + here
                return 0

            return lax.fori_loop(0, PB, band, 0, unroll=4)

        lax.fori_loop(0, PIECES, piece, 0)

    def finish(g, c):
        for p in range(PIECES):
            send_up(g, c, p).wait_send()

        def piece(q, _):
            p = PIECES - 1 - q
            send_down(g, c, p).wait_recv()

            def band(j, _):
                r = p * PB + j
                x, grad = gradient(g, c, r)
                m[c, :, lanes(r)] = m[c, :, lanes(r)] + (step / 2) * grad
                return 0

            lax.fori_loop(0, PB, band, 0, unroll=4)
            store_momentum(c, p).start()
            return 0

        lax.fori_loop(0, PIECES, piece, 0)

    def inner_early(c):
        def band(r, total):
            x = v[c, :, lanes(r)]
            pull = prec[pl.ds(r, 1), :] * (x - obs[pl.ds(r, 1), :])
            mom = m[c, :, lanes(r)] - (step / 2) * (u[c, :, lanes(r)] + pull)
            ahead = next_v[0, c, :, lanes(r)] - mean_next[pl.ds(r, 1), :]
            total = total + (x - mean[1, pl.ds(r, 1), :]) * mom
            return total - (step / 2) * (ahead * u[c, :, lanes(BANDS + r)])

        acc[2, c] = lax.fori_loop(0, BANDS, band, jnp.zeros((CH, SIDE), F32), unroll=4)

    def inner_late(c):
        def band(r, total):
            return total + (v[c, :, lanes(r)] - mean[1, pl.ds(r, 1), :]) * m[c, :, lanes(r)]

        acc[2, c] = lax.fori_loop(0, BANDS, band, jnp.zeros((CH, SIDE), F32), unroll=8)

    def near_copy(slot, d):
        return pltpu.make_async_remote_copy(
            part.at[in_near], part.at[slot], a_send.at[d], a_recv.at[slot], device_id={"rows": near_peer(d)}
        )

    def far_copy(slot, d):
        return pltpu.make_async_remote_copy(
            part_y.at[in_far], part_y.at[slot], b_send.at[d], b_recv.at[slot], device_id={"rows": far_peer(d)}
        )

    def start_sum():
        sub = lax.broadcasted_iota(I32, (CH, SIDE), 0)
        lane = lax.broadcasted_iota(I32, (CH, SIDE), 1)
        inner = jnp.zeros((1, SIDE), F32)
        change = jnp.zeros((1, SIDE), F32)
        for c in range(CHUNKS):
            here = lane == sub + c * CH
            column = jnp.sum(acc[2, c], axis=1, keepdims=True)
            inner += jnp.sum(jnp.where(here, column, 0.0), axis=0, keepdims=True)
            column = jnp.sum(acc[1, c], axis=1, keepdims=True) - jnp.sum(acc[0, c], axis=1, keepdims=True)
            change += jnp.sum(jnp.where(here, column, 0.0), axis=0, keepdims=True)
        own = jnp.concatenate([inner, change, jnp.zeros((6, SIDE), F32)], axis=0)

        part_y[in_far] = own
        for d in range(1, far):
            far_copy(in_far, d).start()
        for d in range(1, far):
            far_copy(lax.rem(in_far + d, far), d).wait_recv()
        total = part_y[0]
        for k in range(1, far):
            total = total + part_y[k]
        part[in_near] = total
        for d in range(1, near):
            near_copy(in_near, d).start()

    def end_sum():
        for d in range(1, near):
            near_copy(lax.rem(in_near + d, near), d).wait_recv()
        total = part[0]
        for k in range(1, near):
            total = total + part[k]
        chees_ref[...] = (
            trajectory_ref[...] * (total[1:2, : CHUNKS * CH] / all_cells) * (total[0:1, : CHUNKS * CH] / all_cells)
        )
        for d in range(1, near):
            near_copy(in_near, d).wait_send()
        for d in range(1, far):
            far_copy(in_far, d).wait_send()

    def stage_of(t, _):
        g = t // CHUNKS
        c = lax.rem(t, CHUNKS)
        upper(g, c)

        @pl.when(g < 2)
        def _():
            move(g, c)
            for p in range(PIECES):
                send_up(g + 1, c, p).start()

            @pl.when(g == 1)
            def _():
                store_position(c).start()

            @pl.when(t == 3)
            def _():
                for d in range(1, ngrp):
                    send_sums(1, d).start()

            for p in range(PIECES):
                send_down(g, c, p).wait_send()

            def again(q, _):
                quarter(g + 1, c, PIECES - 1 - q)
                return 0

            lax.fori_loop(0, PIECES, again, 0)

        @pl.when(t == 4)
        def _():
            means(1)
            send_mean.start()

        @pl.when(t == 5)
        def _():
            send_mean.wait_recv()
            inner_early(1)
            start_sum()

        @pl.when(g == 2)
        def _():
            finish(g, c)

        @pl.when(t == 4)
        def _():
            inner_late(0)
            spread(1)

        return 0

    lax.fori_loop(0, 3 * CHUNKS, stage_of, 0)
    end_sum()

    send_mean.wait_send()
    for which in range(2):
        for d in range(1, ngrp):
            send_sums(which, d).wait_send()
    for c in range(CHUNKS):
        for p in range(PIECES):
            send_down(2, c, p).wait_send()
        store_position(c).wait()
        for p in range(PIECES):
            store_momentum(c, p).wait()


def hand_over(position_ref, momentum_ref, chees_ref, position_out, momentum_out, chees_out, held, in_sem, out_sem):
    part = CHUNKS * CH // STRIPS
    reads, writes = [], []
    for k, (a, b) in enumerate(((position_ref, position_out), (momentum_ref, momentum_out))):
        for i in range(STRIPS):
            rows = pl.ds(i * part, part)
            reads.append(pltpu.make_async_copy(a.at[rows], held.at[k, rows], in_sem.at[k, i]))
            writes.append(pltpu.make_async_copy(held.at[k, rows], b.at[rows], out_sem.at[k, i]))
    for copy in reads:
        copy.start()
    chees_out[...] = chees_ref[...]
    for read, write in zip(reads, writes):
        read.wait()
        write.start()
    for copy in writes:
        copy.wait()


def on_device(start, momenta, observed, precision_obs, blocks, block_cols, block_count, step_size, trajectory):
    nrows = lax.axis_size("rows")
    ngrp = lax.axis_size("grp")
    far = nrows // 8
    hbm = pl.BlockSpec(memory_space=pltpu.HBM)
    vmem = pl.BlockSpec(memory_space=pltpu.VMEM)
    smem = pl.BlockSpec(memory_space=pltpu.SMEM)
    dma = pltpu.SemaphoreType.DMA
    chains = CHUNKS * CH
    position, momentum, chees = pl.pallas_call(
        functools.partial(kernel, nrows, ngrp, chains * ngrp, CELLS * nrows),
        out_shape=(
            jax.ShapeDtypeStruct((chains, CELLS), F32),
            jax.ShapeDtypeStruct((chains, CELLS), F32),
            jax.ShapeDtypeStruct((1, chains), F32),
        ),
        in_specs=[hbm, hbm, hbm, hbm, hbm, vmem, vmem, smem, smem, vmem],
        out_specs=(hbm, hbm, vmem),
        scratch_shapes=[
            pltpu.VMEM((NSTAGE, LOAD * SLOTS, SIDE, SIDE), F32),
            pltpu.VMEM((EDGES, SIDE, 2 * SIDE), BF16),
            pltpu.VMEM((BANDS, SLOTS * SIDE, 2 * SIDE), BF16),
            pltpu.VMEM((CHUNKS, CH, CELLS), F32),
            pltpu.VMEM((CHUNKS, CH, CELLS), F32),
            pltpu.VMEM((CHUNKS, 2 * BANDS, 2 * CH, SIDE), BF16),
            pltpu.VMEM((CHUNKS, CH, 2 * CELLS), F32),
            pltpu.VMEM((PE, CHUNKS * CH, SIDE), F32),
            pltpu.VMEM((2, CHUNKS, CH, CELLS), F32),
            pltpu.VMEM((2, CHUNKS, CH, CELLS), F32),
            pltpu.VMEM((BANDS, SIDE), F32),
            pltpu.VMEM((BANDS, SIDE), F32),
            pltpu.VMEM((2, BANDS, SIDE), F32),
            pltpu.VMEM((2, ngrp, BANDS, SIDE), F32),
            pltpu.VMEM((2, BANDS, SIDE), F32),
            pltpu.VMEM((BANDS, SIDE), F32),
            pltpu.VMEM((3, CHUNKS, CH, SIDE), F32),
            pltpu.VMEM((8, 8, SIDE), F32),
            pltpu.VMEM((far, 8, SIDE), F32),
            pltpu.VMEM((16, SLOTS * BANDS), I32),
            pltpu.SMEM((16, SLOTS * BANDS), I32),
            dma((NSTAGE,)),
            dma((6,)),
            dma((CHUNKS,)),
            dma((CHUNKS, PIECES)),
            dma,
            dma((CHUNKS, PIECES)),
            dma((2, CHUNKS, PIECES)),
            dma((CHUNKS, PIECES)),
            dma((2, CHUNKS, PIECES)),
            dma((2, ngrp)),
            dma((2, ngrp)),
            dma((8,)),
            dma((8,)),
            dma((far,)),
            dma((far,)),
            dma,
            dma,
        ],
        compiler_params=pltpu.CompilerParams(
            collective_id=0, has_side_effects=True, vmem_limit_bytes=60 * 1024 * 1024
        ),
    )(
        start,
        momenta,
        observed.reshape(BANDS, SIDE),
        precision_obs.reshape(BANDS, SIDE),
        blocks.reshape(BANDS * SLOTS, SIDE, SIDE),
        block_cols.T,
        block_count.reshape(1, BANDS),
        block_count,
        step_size,
        trajectory.reshape(1, chains),
    )
    position, momentum, chees = pl.pallas_call(
        hand_over,
        out_shape=(
            jax.ShapeDtypeStruct((chains, CELLS), F32),
            jax.ShapeDtypeStruct((chains, CELLS), F32),
            jax.ShapeDtypeStruct((1, chains), F32),
        ),
        in_specs=[hbm, hbm, vmem],
        out_specs=(hbm, hbm, vmem),
        scratch_shapes=[pltpu.VMEM((2, chains, CELLS), F32), dma((2, STRIPS)), dma((2, STRIPS))],
    )(position, momentum, chees)
    return position, momentum, chees.reshape(chains)


def solution(mesh):
    placed = (
        P("grp", "rows"),
        P("grp", "rows"),
        P("rows"),
        P("rows"),
        P("rows", None, None, None),
        P("rows", None),
        P("rows"),
        P(),
        P("grp"),
    )
    return jax.shard_map(
        on_device,
        mesh=mesh,
        in_specs=placed,
        out_specs=(P("grp", "rows"), P("grp", "rows"), P("grp")),
        check_vma=False,
    )
```

time: 101 us -> 94.3 us (0.934)
  local copies, waits for them, and re-layouts: 5.05 us -> 0 us
  Pallas kernels: 94.1 us -> 92.9 us
    pallas_call x1, Pallas kernels: 94.1 us -> 88.1 us  [on_device(): pl.pallas_call(functools.partial(kernel, nrows, ngrp, chains * ngrp, CELL...]
    unnamed x7 -> x0, local copies, waits for them, and re-layouts: 5.05 us -> none
    pallas_call x0 -> x1, Pallas kernels: none -> 4.76 us  [on_device(): pl.pallas_call(hand_over, out_shape=(jax.ShapeDtypeStruct((chains, CELLS)...]
where the time goes in v1:
time: 94.3 us; the launch traced here: 94.1 us
  Pallas kernels  92.9 us (99%)
  between operations  1.29 us (1%)
    pallas_call x1, Pallas kernels, on_device(): pl.pallas_call(functools.partial(kernel, nrows, ngrp, chains * ngrp, CELL...  88.1 us
    pallas_call x1, Pallas kernels, on_device(): pl.pallas_call(hand_over, out_shape=(jax.ShapeDtypeStruct((chains, CELLS)...  4.76 us

profile of v1, /device:TPU:1, one launch (start us, length us, event | category | flops | bytes accessed | tf_op | source)
XLA Modules:
  0.0 94.1 jit_solution(7089579581586630801)
XLA Ops:
  1.3 88.1 %shard_map.112 = (f32[64,8192]{1,0:T(8,128)}, f32[64,8192]{1,0:T(8,128)}, f32[1,64]{1,0:T(1,128)}) custom-call(f32[64,8192]{1,0:T(8,128)} %start_hbm.1, f32[64,8192]{1,0:T(8,128)} %momenta_hbm.1, f32[64,128]{1,0:T(8,128)} %bitcast.8, f32[64,128]{1,0:T(8,128)} %bitcast.9, f32[256,128,128]{2,1,0:T(8,128)} %bitcast.7, s32[4,64]{1,0:T(4,128)} %bitcast.10, ...), custom_call_target="tpu_custom_call" | custom-call | tf_op jit(solution)/shard_map/pallas_call | solution.py:668
  89.4 4.8 %shard_map.113 = (f32[64,8192]{1,0:T(8,128)}, f32[64,8192]{1,0:T(8,128)}, f32[1,64]{1,0:T(1,128)}) custom-call(f32[64,8192]{1,0:T(8,128)} %get-tuple-element.9.position_ref, f32[64,8192]{1,0:T(8,128)} %get-tuple-element.10.momentum_ref, f32[1,64]{1,0:T(1,128)} %get-tuple-element.11.chees_ref), custom_call_target="tpu_custom_call" | custom-call | tf_op jit(solution)/shard_map/pallas_call | solution.py:732

commit v2 on v1

--- a/solution.py
+++ b/solution.py
@@ -26,7 +26,7 @@
 LOAD = 4
 NLOAD = BANDS // LOAD
 NSTAGE = 4
-STRIPS = 4
+STRIPS = 1
 
 
 def dot(a, b):
@@ -299,7 +299,7 @@
         cell_sums[0, pl.ds(r, 1), :] = total
         return 0
 
-    lax.fori_loop(0, BANDS, first_cells, 0, unroll=4)
+    lax.fori_loop(0, BANDS, first_cells, 0, unroll=8)
     for d in range(1, ngrp):
         send_sums(0, d).start()
 
@@ -327,20 +327,20 @@
 
     to_smem.wait()
 
-    def spread_out(chunks, p):
+    def spread_out(pairs, p):
         def found(r, i):
             x = sums[smem[6 + p, r], i * CH : (i + 1) * CH, :]
             return jnp.where(smem[6 + p, SIDE + r] != 0, x, 0.0)
 
         def fresh(j, _):
             r = p * PB + j
-            for i, c in enumerate(chunks):
+            for i, c in pairs:
                 u[c, :, lanes(r)] = found(r, i)
             return 0
 
         def more(j, _):
             r = p * PB + j
-            for i, c in enumerate(chunks):
+            for i, c in pairs:
                 u[c, :, lanes(r)] = u[c, :, lanes(r)] + found(r, i)
             return 0
 
@@ -366,7 +366,7 @@
         total = joined(dot(split[c, smem[1, place]], flat[smem[0, place]]))
         sums[0, :CH, :] = total
         lax.fori_loop(1, PE, edge, total, unroll=PE - 1)
-        spread_out((c,), p)
+        spread_out(((0, c),), p)
         send_down(g, c, p).start()
 
     def first_quarter(q, _):
@@ -392,9 +392,10 @@
                 )
             return total
 
-        lax.fori_loop(0, PB, edges, jnp.zeros((CHUNKS * CH, SIDE), F32), unroll=8)
-        spread_out(range(CHUNKS), p)
+        lax.fori_loop(0, PB, edges, jnp.zeros((CHUNKS * CH, SIDE), F32), unroll=PB)
+        spread_out(((0, 0),), p)
         send_down(0, 0, p).start()
+        spread_out(((1, 1),), p)
         return 0
 
     lax.fori_loop(0, PIECES, first_quarter, 0)
@@ -430,6 +431,25 @@
 
     step = step_smem[0]
 
+    def inner_here(c, p):
+        def band(j, total):
+            r = p * PB + j
+            x = v[c, :, lanes(r)]
+            pull = prec[pl.ds(r, 1), :] * (x - obs[pl.ds(r, 1), :])
+            mom = m[c, :, lanes(r)] - (step / 2) * (u[c, :, lanes(r)] + pull)
+            return total + (x - mean[1, pl.ds(r, 1), :]) * mom
+
+        old = jnp.where(p == 0, 0.0, acc[2, c])
+        acc[2, c] = lax.fori_loop(0, PB, band, old, unroll=8)
+
+    def inner_ahead(c):
+        def band(r, total):
+            ahead = next_v[0, c, :, lanes(r)] - mean_next[pl.ds(r, 1), :]
+            return total + ahead * u[c, :, lanes(BANDS + r)]
+
+        total = lax.fori_loop(0, BANDS, band, jnp.zeros((CH, SIDE), F32), unroll=8)
+        acc[2, c] = acc[2, c] - (step / 2) * total
+
     def upper(g, c):
         par = lax.rem(g, 2)
 
@@ -450,7 +470,13 @@
                 u[c, :, lanes(r)] = u[c, :, lanes(r)] + term
                 return 0
 
-            return lax.fori_loop(0, PB, row, 0, unroll=PB)
+            lax.fori_loop(0, PB, row, 0, unroll=PB)
+
+            @pl.when((g == 2) & (c == 1))
+            def _():
+                inner_here(1, p)
+
+            return 0
 
         lax.fori_loop(0, PIECES, piece, 0)
 
@@ -505,17 +531,6 @@
             return 0
 
         lax.fori_loop(0, PIECES, piece, 0)
-
-    def inner_early(c):
-        def band(r, total):
-            x = v[c, :, lanes(r)]
-            pull = prec[pl.ds(r, 1), :] * (x - obs[pl.ds(r, 1), :])
-            mom = m[c, :, lanes(r)] - (step / 2) * (u[c, :, lanes(r)] + pull)
-            ahead = next_v[0, c, :, lanes(r)] - mean_next[pl.ds(r, 1), :]
-            total = total + (x - mean[1, pl.ds(r, 1), :]) * mom
-            return total - (step / 2) * (ahead * u[c, :, lanes(BANDS + r)])
-
-        acc[2, c] = lax.fori_loop(0, BANDS, band, jnp.zeros((CH, SIDE), F32), unroll=4)
 
     def inner_late(c):
         def band(r, total):
@@ -609,7 +624,7 @@
         @pl.when(t == 5)
         def _():
             send_mean.wait_recv()
-            inner_early(1)
+            inner_ahead(1)
             start_sum()
 
         @pl.when(g == 2)

time: 94.3 us -> 94 us (level)
  no operation moved by 1% of the time
where the time goes in v2:
time: 94 us; the launch traced here: 93.8 us
  Pallas kernels  92.5 us (98%)
  between operations  1.29 us (1%)
    pallas_call x1, Pallas kernels, on_device(): pl.pallas_call(functools.partial(kernel, nrows, ngrp, chains * ngrp, CELL...  87.7 us
    pallas_call x1, Pallas kernels, on_device(): pl.pallas_call(hand_over, out_shape=(jax.ShapeDtypeStruct((chains, CELLS)...  4.82 us

profile of v2, /device:TPU:1, one launch (start us, length us, event | category | flops | bytes accessed | tf_op | source)
XLA Modules:
  0.0 93.8 jit_solution(10549990411953781002)
XLA Ops:
  1.3 87.7 %shard_map.112 = (f32[64,8192]{1,0:T(8,128)}, f32[64,8192]{1,0:T(8,128)}, f32[1,64]{1,0:T(1,128)}) custom-call(f32[64,8192]{1,0:T(8,128)} %start_hbm.1, f32[64,8192]{1,0:T(8,128)} %momenta_hbm.1, f32[64,128]{1,0:T(8,128)} %bitcast.8, f32[64,128]{1,0:T(8,128)} %bitcast.9, f32[256,128,128]{2,1,0:T(8,128)} %bitcast.7, s32[4,64]{1,0:T(4,128)} %bitcast.10, ...), custom_call_target="tpu_custom_call" | custom-call | tf_op jit(solution)/shard_map/pallas_call | solution.py:683
  89.0 4.8 %shard_map.113 = (f32[64,8192]{1,0:T(8,128)}, f32[64,8192]{1,0:T(8,128)}, f32[1,64]{1,0:T(1,128)}) custom-call(f32[64,8192]{1,0:T(8,128)} %get-tuple-element.9.position_ref, f32[64,8192]{1,0:T(8,128)} %get-tuple-element.10.momentum_ref, f32[1,64]{1,0:T(1,128)} %get-tuple-element.11.chees_ref), custom_call_target="tpu_custom_call" | custom-call | tf_op jit(solution)/shard_map/pallas_call | solution.py:747

commit v3 on v2

--- a/solution.py
+++ b/solution.py
@@ -26,7 +26,7 @@
 LOAD = 4
 NLOAD = BANDS // LOAD
 NSTAGE = 4
-STRIPS = 1
+STRIPS = 2
 
 
 def dot(a, b):
@@ -413,17 +413,14 @@
             total = total + cell_all[which, k]
         mean[which] = total / chain_total
 
-    def spread(which):
-        for c in range(CHUNKS):
-
-            def add(r, total):
-                x = v[c, :, lanes(r)] - mean[which, pl.ds(r, 1), :]
-                return total + x * x
-
-            acc[which, c] = lax.fori_loop(0, BANDS, add, jnp.zeros((CH, SIDE), F32), unroll=8)
+    def spread(which, c):
+        def add(r, total):
+            x = v[c, :, lanes(r)] - mean[which, pl.ds(r, 1), :]
+            return total + x * x
+
+        acc[which, c] = lax.fori_loop(0, BANDS, add, jnp.zeros((CH, SIDE), F32), unroll=8)
 
     means(0)
-    spread(0)
     for c in range(CHUNKS):
         load_m(c).wait()
     load_obs.wait()
@@ -590,6 +587,10 @@
     def stage_of(t, _):
         g = t // CHUNKS
         c = lax.rem(t, CHUNKS)
+        @pl.when(g == 0)
+        def _():
+            spread(0, c)
+
         upper(g, c)
 
         @pl.when(g < 2)
@@ -634,7 +635,8 @@
         @pl.when(t == 4)
         def _():
             inner_late(0)
-            spread(1)
+            for k in range(CHUNKS):
+                spread(1, k)
 
         return 0
 

time: 94 us -> 93.7 us (level)
  no operation moved by 1% of the time
where the time goes in v3:
time: 93.7 us; the launch traced here: 93.5 us
  Pallas kernels  92.2 us (98%)
  between operations  1.29 us (1%)
    pallas_call x1, Pallas kernels, on_device(): pl.pallas_call(functools.partial(kernel, nrows, ngrp, chains * ngrp, CELL...  87.7 us
    pallas_call x1, Pallas kernels, on_device(): pl.pallas_call(hand_over, out_shape=(jax.ShapeDtypeStruct((chains, CELLS)...  4.48 us

profile of v3, /device:TPU:1, one launch (start us, length us, event | category | flops | bytes accessed | tf_op | source)
XLA Modules:
  0.0 93.5 jit_solution(15629129493301451186)
XLA Ops:
  1.3 87.7 %shard_map.112 = (f32[64,8192]{1,0:T(8,128)}, f32[64,8192]{1,0:T(8,128)}, f32[1,64]{1,0:T(1,128)}) custom-call(f32[64,8192]{1,0:T(8,128)} %start_hbm.1, f32[64,8192]{1,0:T(8,128)} %momenta_hbm.1, f32[64,128]{1,0:T(8,128)} %bitcast.8, f32[64,128]{1,0:T(8,128)} %bitcast.9, f32[256,128,128]{2,1,0:T(8,128)} %bitcast.7, s32[4,64]{1,0:T(4,128)} %bitcast.10, ...), custom_call_target="tpu_custom_call" | custom-call | tf_op jit(solution)/shard_map/pallas_call | solution.py:685
  89.0 4.5 %shard_map.113 = (f32[64,8192]{1,0:T(8,128)}, f32[64,8192]{1,0:T(8,128)}, f32[1,64]{1,0:T(1,128)}) custom-call(f32[64,8192]{1,0:T(8,128)} %get-tuple-element.9.position_ref, f32[64,8192]{1,0:T(8,128)} %get-tuple-element.10.momentum_ref, f32[1,64]{1,0:T(1,128)} %get-tuple-element.11.chees_ref), custom_call_target="tpu_custom_call" | custom-call | tf_op jit(solution)/shard_map/pallas_call | solution.py:749
